TPU v7x, 32 devices: a whole 2x2x4 slice. The times are simulated.
32 devices in a mesh: parts: 2 (over y), seq: 4 (over z), head: 4 (over x, core).
Axes of the slice: x: 2, y: 2, z: 4, core: 2. Of those that a mesh axis runs over, the one named last changes fastest.
Arguments:
- hidden: bfloat16 [48, 12288], P(('parts', 'head'), 'seq'), parts along dimension 0, may hold values from -600 to 600
- norm_gain: float32 [12288], P('seq'), may hold values from 0.1 to 1.9
- w_query: bfloat16 [12288, 12288], P('seq', 'head'), may hold values from -0.0546875 to 0.0546875
- w_key: bfloat16 [12288, 1024], P('seq', 'head'), may hold values from -0.0546875 to 0.0546875
- w_value: bfloat16 [12288, 1024], P('seq', 'head'), may hold values from -0.0546875 to 0.0546875
- w_out: bfloat16 [12288, 12288], P('head', 'seq'), may hold values from -0.0546875 to 0.0546875
- lengths: int32 [48], P('parts'), parts along dimension 0, may hold values from 1 to 512, as said below
- key_cache: bfloat16 [48, 8, 512, 128], P('parts', 'head', 'seq'), parts along dimension 0, may hold values from -600 to 600, as said below
- value_cache: bfloat16 [48, 8, 512, 128], P('parts', 'head', 'seq'), parts along dimension 0, may hold values from -6 to 6
Outputs:
- attn_out: bfloat16 [48, 12288], P(('parts', 'head'), 'seq'), parts along dimension 0
There are 2 independent parts, one for each index of `parts`. A program takes and returns all parts, laid end to end along the dimension named above; an argument that names none is the same for every part. Nothing has to cross between parts.
Inputs may be any that keep to these rules, and one draw needn't show every extreme that they name: Sequence b holds lengths[b] cached tokens at positions 0 to lengths[b] - 1; its new token takes position lengths[b]. `key_cache`: positions at or past a sequence's length hold no data.
All inputs are finite; a program needn't handle non-finite values.
Results may differ from a plain program's by a relative error of at most 0.0075.
The roundings to bfloat16 on the way count: a program that leaves them out, or rounds other values in their place, can miss the bound.
Values may be sent and summed in bfloat16 or wider, within the bound.
A program may use at most 128 MiB of HBM per device.

v0:
```python
import jax
import jax.numpy as jnp
from jax import lax
from jax.sharding import PartitionSpec as P

D = 12288


EPSILON = 1e-05


def joined(value, axis, join):
    pieces = jax.tree.map(lambda part: lax.all_gather(part, axis), value)
    head = jax.tree.map(lambda part: part[0], pieces)
    tail = jax.tree.map(lambda part: part[1:], pieces)
    subtotal, _ = lax.scan(lambda subtotal, slab: (join(subtotal, slab), None), head, tail)
    return subtotal


def join_parts(earlier, later):
    new_max = jnp.maximum(earlier[0], later[0])
    left_factor = jnp.exp(earlier[0] - new_max)
    right_factor = jnp.exp(later[0] - new_max)
    den_total = earlier[1] * left_factor + later[1] * right_factor
    acc_total = earlier[2] * left_factor[..., None] + later[2] * right_factor[..., None]
    return (new_max, den_total, acc_total)


def local(hidden, norm_gain, w_query, w_key, w_value, w_out, lengths, key_cache, value_cache):
    batch_size, kv_local, block_len, head_size = key_cache.shape
    group_size = w_query.shape[1] // (kv_local * head_size)
    token_rows = lax.all_gather(hidden, "head", axis=0, tiled=True)
    widened = token_rows.astype(jnp.float32)
    square_local = jnp.sum(widened * widened, axis=1)
    scaled = (widened * norm_gain).astype(jnp.bfloat16)
    query_part = jnp.dot(scaled, w_query, preferred_element_type=jnp.float32)
    key_part = jnp.dot(scaled, w_key, preferred_element_type=jnp.float32)
    value_part = jnp.dot(scaled, w_value, preferred_element_type=jnp.float32)
    query_factor = float(head_size) ** (-0.5)
    norm_total = lax.psum(square_local, "seq")
    query_sum, key_sum, value_sum = lax.psum((query_part, key_part, value_part), "seq")
    inverse_rms = lax.rsqrt(norm_total / D + EPSILON)[:, None]
    queries = (query_sum * inverse_rms * query_factor).astype(jnp.bfloat16)
    new_keys = (key_sum * inverse_rms).astype(jnp.bfloat16)
    new_values = (value_sum * inverse_rms).astype(jnp.bfloat16)
    grouped = queries.reshape(batch_size, kv_local, group_size, head_size)
    scores = jnp.einsum("bkgd,bkpd->bkgp", grouped, key_cache, preferred_element_type=jnp.float32)
    offset = lax.axis_index("seq") * block_len
    positions = offset + jnp.arange(block_len, dtype=jnp.int32)
    live_mask = (positions[None, :] < lengths[:, None])[:, None, None, :]
    block_max = jnp.max(jnp.where(live_mask, scores, -1e30), axis=-1)
    shifted = jnp.where(live_mask, scores - block_max[..., None], 0.0)
    weights = jnp.where(live_mask, jnp.exp(shifted), 0.0).astype(jnp.bfloat16)
    block_den = jnp.sum(weights.astype(jnp.float32), axis=-1)
    block_acc = jnp.einsum(
        "bkgp,bkpd->bkgd", weights, value_cache, preferred_element_type=jnp.float32
    )
    self_score = jnp.einsum(
        "oips,ois->oip",
        grouped,
        new_keys.reshape(batch_size, kv_local, head_size),
        preferred_element_type=jnp.float32,
    )
    global_max, den_merged, acc_merged = joined(
        (block_max, block_den, block_acc), "seq", join_parts
    )
    top_score = jnp.maximum(global_max, self_score)
    factors = jnp.exp(global_max - top_score)
    den_sum = den_merged * factors
    acc_sum = acc_merged * factors[..., None]
    own_weight = jnp.exp(self_score - top_score)
    denominator = den_sum + own_weight
    numerator = acc_sum + own_weight[..., None] * new_values.reshape(
        batch_size, kv_local, 1, head_size
    ).astype(jnp.float32)
    mixed = (
        (numerator / denominator[..., None])
        .astype(jnp.bfloat16)
        .reshape(batch_size, kv_local * group_size * head_size)
    )
    output = lax.psum_scatter(
        jnp.dot(mixed, w_out, preferred_element_type=jnp.float32),
        "head",
        scatter_dimension=0,
        tiled=True,
    )
    return output.astype(jnp.bfloat16)


def solution(mesh):
    return jax.shard_map(
        local,
        mesh=mesh,
        in_specs=(
            P(("parts", "head"), "seq"),
            P("seq"),
            P("seq", "head"),
            P("seq", "head"),
            P("seq", "head"),
            P("head", "seq"),
            P("parts"),
            P("parts", "head", "seq", None),
            P("parts", "head", "seq", None),
        ),
        out_specs=P(("parts", "head"), "seq"),
        check_vma=False,
    )
```

profile of v0, /device:TPU:0, one launch (start us, length us, event | category | flops | bytes accessed | tf_op | source)
XLA Modules:
  0.0 131.4 jit_solution(6576906076258920298)
XLA Ops:
  6.5 7.2 %all-gather.3 = bf16[4,6,3072]{2,1,0:T(8,128)(2,1)S(1)} all-gather(bf16[1,6,3072]{2,1,0:T(8,128)(2,1)} %bitcast.49), channel_id=1, replica_groups=mesh['parts'=2,'seq'=4,'head'=4] {'head'}, dimensions={0}, use_global_device_ids=true | all-gather | bytes 184320 | tf_op jit(solution)/shard_map/all_gather | solution.py:32
  13.8 0.9 multiply_reduce_fusion
  14.6 9.8 %fusion.12 = f32[24,3072]{1,0:T(8,128)} fusion(bf16[24,3072]{1,0:T(8,128)(2,1)S(1)} %get-tuple-element.86, bf16[3072,3072]{1,0:T(8,128)(2,1)} %param.13), kind=kOutput, calls=%fused_computation.30 | convolution fusion | flops 452984832 | bytes 19316736 | tf_op jit(solution)/shard_map/dot_general | solution.py:36
  24.5 0.3 fusion.15
  24.8 1.1 copy-done.2
  25.9 0.3 fusion.13
  26.2 21.2 %all-reduce.2 = (f32[24]{0:T(128)S(1)}, f32[24,256]{1,0:T(8,128)S(1)}, f32[24,256]{1,0:T(8,128)S(1)}) all-reduce(f32[24]{0:T(128)S(1)} %get-tuple-element.85, f32[24,256]{1,0:T(8,128)S(1)} %fusion.13, f32[24,256]{1,0:T(8,128)S(1)} %fusion.15), channel_id=1, replica_groups=mesh['parts'=2,'seq'=4,'head'=4] {'seq'}, use_global_device_ids=true, to_apply=%region_2.0 | all-reduce | flops 12312 | bytes 98496 | tf_op jit(solution)/shard_map/psum | solution.py:40
  47.4 0.1 broadcast_compare_fusion
  47.5 15.1 %all-reduce.5.cloned.1.call-done = f32[24,3072]{1,0:T(8,128)} async-done(((f32[24,3072]{1,0:T(8,128)}), f32[24,3072]{1,0:T(8,128)}) %all-reduce.5.cloned.1.call-update) | async-done | bytes 294928 | tf_op jit(solution)/shard_map/psum | solution.py:41
  62.6 1.1 multiply_convert_fusion
  63.7 0.1 reshape.54
  63.8 1.0 select_reduce_fusion
  64.8 2.0 %fusion.8 = f32[24,2,12,128]{3,2,1,0:T(8,128)S(1)} fusion(bf16[24,2,128,128]{3,2,1,0:T(8,128)(2,1)} %param.19, f32[24,2,12,128]{3,2,1,0:T(8,128)S(1)} %get-tuple-element.90, f32[24,2,12]{2,1,0:T(2,128)S(1)} %get-tuple-element.89, pred[24,128]{1,0:T(8,128)(4,1)S(1)} %broadcast_compare_fusion), kind=kOutput, calls=%fused_computation.29 | convolution fusion | flops 19169280 | bytes 2168064 | tf_op jit(solution)/shard_map/bkgp,bkpd->bkgd/dot_general | solution.py:55
  66.8 0.9 copy.26
  67.7 0.1 fusion.7
  67.9 13.7 %all-gather = f32[96,2,12]{2,1,0:T(2,128)S(1)} all-gather(f32[24,2,12]{2,1,0:T(2,128)S(1)} %get-tuple-element.89), channel_id=2, replica_groups=mesh['parts'=2,'seq'=4,'head'=4] {'seq'}, dimensions={0}, use_global_device_ids=true | all-gather | bytes 11520 | tf_op jit(solution)/shard_map/all_gather | solution.py:13
  81.5 0.4 convert_reduce_fusion
  81.9 14.2 %all-gather.1 = f32[96,2,12]{2,1,0:T(2,128)S(1)} all-gather(f32[24,2,12]{2,1,0:T(2,128)S(1)} %convert_reduce_fusion), channel_id=3, replica_groups=mesh['parts'=2,'seq'=4,'head'=4] {'seq'}, dimensions={0}, use_global_device_ids=true | all-gather | bytes 11520 | tf_op jit(solution)/shard_map/all_gather | solution.py:13
  96.1 0.2 fusion.14
  96.3 0.1 copy.39
  96.4 0.1 copy.29
  96.5 0.1 copy.32
  96.6 0.1 copy.30
  96.7 0.1 copy.33
  96.8 2.9 %all-gather.6.cloned.1.call-done = f32[96,2,12,128]{3,1,2,0:T(2,128)} async-done(((f32[24,2,12,128]{3,1,2,0:T(2,128)}), f32[96,2,12,128]{3,1,2,0:T(2,128)}) %all-gather.6.cloned.1.call-update) | async-done | bytes 1179664 | tf_op jit(solution)/shard_map/all_gather | solution.py:13
  99.8 1.1 slice.32
  100.9 0.1 slice-done
  101.0 2.0 %while.14 = (s32[]{:T(128)}, f32[24,2,12]{0,1,2:T(2,128)S(1)}, f32[24,2,12]{0,1,2:T(2,128)S(1)}, f32[24,2,12,128]{3,2,1,0:T(8,128)S(1)}, f32[3,24,2,12]{1,2,3,0:...) while((s32[]{:T(128)}, f32[24,2,12]{0,1,2:T(2,128)S(1)}, ...), condition=%wide.region_6.7_spmd, body=%wide.region_5.6_spmd.sunk | while | flops 224642 | bytes 1506917 | solution.py:16
  101.1 0.1 copy.54
  101.2 0.1 copy.55
  101.3 0.4 fusion.33
  101.7 0.1 copy.54
  101.8 0.1 copy.55
  101.9 0.4 fusion.33
  102.4 0.1 copy.54
  102.5 0.1 copy.55
  102.6 0.4 fusion.33
  103.0 0.1 copy.37
  103.1 0.1 copy.35
  103.2 0.1 copy.36
  103.3 0.4 divide_convert_fusion
  103.7 0.1 reshape.56
  103.8 7.7 %fusion.16 = f32[24,3072]{1,0:T(8,128)S(1)} fusion(bf16[24,3072]{1,0:T(8,128)(2,1)S(1)} %reshape.56, bf16[3072,3072]{1,0:T(8,128)(2,1)} %param.16), kind=kOutput, calls=%fused_computation.34 | convolution fusion | flops 452984832 | bytes 19316736 | tf_op jit(solution)/shard_map/dot_general | solution.py:82
  111.5 9.6 %fusion = f32[8,3072]{1,0:T(8,128)S(1)} fusion(f32[24,3072]{1,0:T(8,128)S(1)} %fusion.16), kind=kCustom, calls=%all-reduce-scatter | all-reduce-scatter fusion | flops 98305 | bytes 393728
  121.2 1.3 collective-permute-start
  122.5 0.6 dynamic-slice.4
  123.8 0.2 concatenate
  123.9 0.6 dynamic-slice_convert_fusion
  (33 shorter events, 0.5 us)
Async XLA Ops:
  6.5 57.3 %copy-start = (bf16[24,2,128,128]{3,2,1,0:T(8,128)(2,1)S(1)}, bf16[24,2,128,128]{3,2,1,0:T(8,128)(2,1)}, u32[]{:S(2)}) copy-start(bf16[24,2,128,128]{3,2,1,0:T(8,128)(2,1)} %param.18) | copy-start | bytes 4718596
  6.5 56.1 %all-reduce.5.cloned.1.call-start = ((), (), s32[]{:S(2)}) async-start(), calls=%async_computation | async-start | bytes 589824 | tf_op jit(solution)/shard_map/psum | solution.py:41
  14.6 9.8 %copy-start.1 = (bf16[3072,256]{1,0:T(8,128)(2,1)S(1)}, bf16[3072,256]{1,0:T(8,128)(2,1)}, u32[]{:S(2)}) copy-start(bf16[3072,256]{1,0:T(8,128)(2,1)} %param.15) | copy-start | bytes 4718596
  24.4 75.3 %all-gather.6.cloned.1.call-start = ((), (), s32[]{:S(2)}) async-start(), calls=%async_computation.1 | async-start | bytes 1474560 | tf_op jit(solution)/shard_map/all_gather | solution.py:13
  24.5 1.4 %copy-start.2 = (bf16[3072,256]{1,0:T(8,128)(2,1)S(1)}, bf16[3072,256]{1,0:T(8,128)(2,1)}, u32[]{:S(2)}) copy-start(bf16[3072,256]{1,0:T(8,128)(2,1)} %param.14) | copy-start | bytes 4718596
  24.5 22.9 %copy-start.4 = (s32[24]{0:T(128)S(1)}, s32[24]{0:T(128)}, u32[]{:S(2)}) copy-start(s32[24]{0:T(128)} %param.17) | copy-start | bytes 292
  99.8 1.3 slice-start
  103.8 18.7 %copy-start.3 = (u32[32]{0:T(128)S(1)}, u32[32]{0:T(128)}, u32[]{:S(2)}) copy-start(u32[32]{0:T(128)} %constant.37) | copy-start | bytes 388
  121.2 2.6 %collective-permute-start = (bf16[6,3072]{1,0:T(8,128)(2,1)S(1)}, bf16[6,3072]{1,0:T(8,128)(2,1)S(1)}, u32[]{:S(2)}, u32[]{:S(2)}) collective-permute-start(bf16[6,3072]{1,0:T(8,128)(2,1)S(1)} %slice.36), channel_id=1, source_target_pairs={{0,1},{1,2},{2,3},{4,5},{5,6},{6,7},{8,9},{9,10},{10,11},{12,13},{... | collective-permute-start | bytes 110600
Sparse Core Ops, SparseCore 0:
  24.5 38.0 all-reduce.4
  67.9 31.8 all-gather.5
where the time goes:
time: 133 us; the launch traced here: 131 us
  blocking collectives  65.9 us (50%)
  matrix products  21.3 us (16%)
  waiting for transfers between devices  18.1 us (14%)
  between operations  14.3 us (11%)
  local copies, waits for them, and re-layouts  6.41 us (5%)
  other arithmetic  4.09 us (3%)
  starting transfers between devices  1.34 us (1%)
    all_gather x2, blocking collectives, joined(): pieces = jax.tree.map(lambda part: lax.all_gather(part, axis), value)  27.8 us
    psum x1, blocking collectives, local(): norm_total = lax.psum(square_local, 'seq')  21.2 us
    psum x1, waiting for transfers between devices, local(): lax.psum((query_part, key_part, value_part), 'seq')  15.1 us
    dot_general x1, matrix products, local(): query_part = jnp.dot(scaled, w_query, preferred_element_type=jnp.float32)  9.76 us
    unnamed x1, blocking collectives  9.65 us
    dot_general x1, matrix products, local(): jnp.dot(mixed, w_out, preferred_element_type=jnp.float32)  7.7 us
    all_gather x1, blocking collectives, local(): token_rows = lax.all_gather(hidden, 'head', axis=0, tiled=True)  7.19 us
    all_gather x1, waiting for transfers between devices, joined(): pieces = jax.tree.map(lambda part: lax.all_gather(part, axis), value)  2.93 us
  transfers between devices with their start and end apart: 3, of which 2 were waited for; matrix products, arithmetic and copies ran while one was open for 2% of the time, Pallas kernels for 0%

commit v1 on v0

--- a/solution.py
+++ b/solution.py
@@ -1,6 +1,10 @@
+import functools
+
 import jax
 import jax.numpy as jnp
 from jax import lax
+from jax.experimental import pallas as pl
+from jax.experimental.pallas import tpu as pltpu
 from jax.sharding import PartitionSpec as P
 
 D = 12288
@@ -87,9 +91,340 @@
     return output.astype(jnp.bfloat16)
 
 
+MESH = pl.DeviceIdType.MESH
+
+
+def layer_kernel(
+    n_seq, n_head, hid, gain, lens, wq, wk, wv, wo, kc, vc, out,
+    hid_buf, x_scr, xs_scr, len_scr, wq_buf, wkv_buf, wo_buf, kc_buf, vc_buf,
+    part, rs_buf, ag_buf, q_scr, sc_scr, acc_scr, st_buf, ra_buf, mix_buf, o_acc, o_send, o_recv,
+    load_sem, hid_send, hid_recv, rs_send, rs_recv, ag_send, ag_recv,
+    st_send, st_recv, ra_send, ra_recv, mx_send, mx_recv, os_sem, or_sem,
+):
+    f32, bf16 = jnp.float32, jnp.bfloat16
+    seq, hd = lax.axis_index("seq"), lax.axis_index("head")
+    rows, feat = hid.shape
+    batch, kv, block, size = kc.shape
+    heads = wq.shape[1] // size
+    group = heads // kv
+    own = heads // n_seq
+    width = own * size
+    tile = 256 if width % 256 == 0 else size
+    kv_cols = kv * size
+
+    def load(index, source, target):
+        copy = pltpu.make_async_copy(source, target, load_sem.at[index])
+        copy.start()
+        return copy
+
+    def to(axis, index, source, target, send, recv):
+        return pltpu.make_async_remote_copy(
+            src_ref=source, dst_ref=target, send_sem=send, recv_sem=recv,
+            device_id={axis: index}, device_id_type=MESH,
+        )
+
+    seq_to = [lax.rem(seq + j + 1, n_seq) for j in range(n_seq)]
+    seq_from = [lax.rem(seq + n_seq - j - 1, n_seq) for j in range(n_seq)]
+    head_to = [lax.rem(hd + j + 1, n_head) for j in range(n_head)]
+
+    own_hidden = load(0, hid, hid_buf.at[hd])
+    key_load = load(1, wk, wkv_buf.at[:, pl.ds(0, kv_cols)])
+    value_load = load(2, wv, wkv_buf.at[:, pl.ds(kv_cols, kv_cols)])
+    q_loads = [
+        load(3 + j, wq.at[:, pl.ds(pl.multiple_of(seq_to[j] * width, width), width)], wq_buf.at[j])
+        for j in range(n_seq)
+    ]
+    base = 3 + n_seq
+    kc_load = load(base, kc, kc_buf)
+    vc_load = load(base + 1, vc, vc_buf)
+    o_loads = [
+        load(base + 2 + j, wo.at[pl.ds(j * width, width)], wo_buf.at[j]) for j in range(n_seq)
+    ]
+
+    barrier = pltpu.get_barrier_semaphore()
+    for j in range(n_head - 1):
+        pl.semaphore_signal(barrier, inc=1, device_id={"head": head_to[j]}, device_id_type=MESH)
+    for j in range(n_seq - 1):
+        pl.semaphore_signal(barrier, inc=1, device_id={"seq": seq_to[j]}, device_id_type=MESH)
+    pl.semaphore_wait(barrier, n_head + n_seq - 2)
+
+    hid_copies = [
+        to("head", head_to[j], hid, hid_buf.at[hd], hid_send.at[j], hid_recv.at[j])
+        for j in range(n_head - 1)
+    ]
+    for copy in hid_copies:
+        copy.start()
+    for b in range(batch):
+        len_scr[b : b + 1, :] = jnp.full((1, block), lens[b], jnp.int32)
+    own_hidden.wait()
+    for copy in hid_copies:
+        copy.wait_recv()
+    for j in range(n_head):
+        x_scr[j * rows : (j + 1) * rows, :] = hid_buf[j].astype(f32)
+    widened = x_scr[...]
+    square = jnp.sum(widened * widened, axis=1, keepdims=True)
+    xs_scr[...] = (widened * gain[...]).astype(bf16)
+
+    key_load.wait()
+    value_load.wait()
+    rs_copies = []
+    for j in range(n_seq):
+        q_loads[j].wait()
+
+        @pl.loop(0, width // tile)
+        def _(n):
+            cols = pl.ds(pl.multiple_of(n * tile, tile), tile)
+            part[j, :, cols] = jnp.dot(xs_scr[...], wq_buf[j, :, cols], preferred_element_type=f32)
+
+        kv_at = pl.ds(pl.multiple_of(seq_to[j] * size, size), size)
+        part[j, :, width : width + size] = jnp.dot(
+            xs_scr[...], wkv_buf[:, kv_at], preferred_element_type=f32
+        )
+        part[j, :, width + size :] = jnp.broadcast_to(square, (batch, 128))
+        if j < n_seq - 1:
+            copy = to("seq", seq_to[j], part.at[j], rs_buf.at[j], rs_send.at[j], rs_recv.at[j])
+            copy.start()
+            rs_copies.append(copy)
+
+    for copy in rs_copies:
+        copy.wait_recv()
+
+    def summed(cols):
+        total = part[n_seq - 1, :, cols]
+        for j in range(n_seq - 1):
+            total = total + rs_buf[j, :, cols]
+        return total
+
+    mean_square = summed(slice(width + size, width + size + 128)) / (feat * n_seq)
+    inverse_rms = lax.rsqrt(mean_square + EPSILON)[:, :1]
+    factor = float(size) ** (-0.5)
+    ag_buf[seq, :, :width] = (summed(slice(0, width)) * inverse_rms * factor).astype(bf16)
+    ag_buf[seq, :, width:] = (summed(slice(width, width + size)) * inverse_rms).astype(bf16)
+    ag_copies = []
+    for j in range(n_seq - 1):
+        copy = to("seq", seq_to[j], ag_buf.at[seq], ag_buf.at[seq], ag_send.at[j], ag_recv.at[j])
+        copy.start()
+        ag_copies.append(copy)
+    kc_load.wait()
+    vc_load.wait()
+    for copy in ag_copies:
+        copy.wait_recv()
+    for s in range(n_seq):
+        for i in range(own):
+            at = (s * own + i) * batch
+            q_scr[at : at + batch, :] = ag_buf[s, :, i * size : (i + 1) * size].astype(f32)
+
+    unroll = 4 if batch % 4 == 0 else 1
+
+    @pl.loop(0, batch // unroll)
+    def _(step):
+        for u in range(unroll):
+            b = step * unroll + u
+            for k in range(kv):
+                at = pl.ds(k * group * batch + b, group, stride=batch)
+                sc_scr[at, :] = lax.dot_general(
+                    q_scr[at, :].astype(bf16), kc_buf[b, k], (((1,), (1,)), ((), ())),
+                    preferred_element_type=f32,
+                )
+
+    lane = lax.broadcasted_iota(jnp.int32, (batch, block), 1)
+    live = lane + seq * block < len_scr[...]
+    stats = jnp.zeros((batch, 128), f32)
+    for h in range(heads):
+        scores = sc_scr[h * batch : (h + 1) * batch, :]
+        top = jnp.max(jnp.where(live, scores, -1e30), axis=1, keepdims=True)
+        shifted = jnp.where(live, scores - top, 0.0)
+        weights = jnp.where(live, jnp.exp(shifted), 0.0).astype(bf16).astype(f32)
+        sc_scr[h * batch : (h + 1) * batch, :] = weights
+        total = jnp.sum(weights, axis=1, keepdims=True)
+        stats = jnp.where(lane == h, top, jnp.where(lane == 64 + h, total, stats))
+    st_buf[n_seq - 1] = stats
+    st_copies = []
+    for j in range(n_seq - 1):
+        copy = to("seq", seq_to[j], st_buf.at[n_seq - 1], st_buf.at[j], st_send.at[j], st_recv.at[j])
+        copy.start()
+        st_copies.append(copy)
+
+    @pl.loop(0, batch // unroll)
+    def _(step):
+        for u in range(unroll):
+            b = step * unroll + u
+            for k in range(kv):
+                at = pl.ds(k * group * batch + b, group, stride=batch)
+                acc_scr[at, :] = jnp.dot(
+                    sc_scr[at, :].astype(bf16), vc_buf[b, k], preferred_element_type=f32
+                )
+
+    ra_copies = []
+    part_rows = own * batch
+    for j in range(n_seq - 1):
+        at = pl.ds(pl.multiple_of(seq_to[j] * part_rows, part_rows), part_rows)
+        copy = to("seq", seq_to[j], acc_scr.at[at], ra_buf.at[j], ra_send.at[j], ra_recv.at[j])
+        copy.start()
+        ra_copies.append(copy)
+
+    kv_head = (seq * own) // group
+    new_key = ag_buf[kv_head, :, width:].astype(f32)
+    new_value = ag_buf[kv + kv_head, :, width:].astype(f32)
+    own_at = pl.multiple_of(seq * part_rows, part_rows)
+    self_score = jnp.zeros((batch, 128), f32)
+    for i in range(own):
+        query = q_scr[pl.ds(own_at + i * batch, batch), :]
+        score = jnp.sum(query * new_key, axis=1, keepdims=True)
+        self_score = jnp.where(lane == i, score, self_score)
+    for copy in st_copies:
+        copy.wait_recv()
+    shift = lax.rem(128 - seq * own, 128)
+    maxes = [pltpu.roll(st_buf[j], shift, 1) for j in range(n_seq)]
+    dens = [pltpu.roll(m, 64, 1) for m in maxes]
+    top_score = self_score
+    for m in maxes:
+        top_score = jnp.maximum(top_score, m)
+    factors = [jnp.exp(m - top_score) for m in maxes]
+    own_weight = jnp.exp(self_score - top_score)
+    denominator = own_weight
+    for f, d in zip(factors, dens):
+        denominator = denominator + f * d
+    own_weight = own_weight / denominator
+    factors = [f / denominator for f in factors]
+    for copy in ra_copies:
+        copy.wait_recv()
+    for i in range(own):
+        mixed = own_weight[:, i : i + 1] * new_value
+        mixed += factors[n_seq - 1][:, i : i + 1] * acc_scr[pl.ds(own_at + i * batch, batch), :]
+        for j in range(n_seq - 1):
+            mixed += factors[j][:, i : i + 1] * ra_buf[j, i * batch : (i + 1) * batch, :]
+        mix_buf[seq, :, i * size : (i + 1) * size] = mixed.astype(bf16)
+    mx_copies = []
+    for j in range(n_seq - 1):
+        copy = to("seq", seq_to[j], mix_buf.at[seq], mix_buf.at[seq], mx_send.at[j], mx_recv.at[j])
+        copy.start()
+        mx_copies.append(copy)
+    for copy in o_loads:
+        copy.wait()
+
+    columns = wo.shape[1]
+    o_tile = 256 if columns % (4 * 256) == 0 else 128
+    chunks = 4 if columns % (4 * o_tile) == 0 else 1
+    chunk = columns // chunks
+    order = [seq] + seq_from[: n_seq - 1]
+    o_copies = []
+    for j in range(n_seq):
+        if j > 0:
+            mx_copies[j - 1].wait_recv()
+        source = order[j]
+        if j < n_seq - 1:
+
+            @pl.loop(0, columns // o_tile)
+            def _(n):
+                cols = pl.ds(pl.multiple_of(n * o_tile, o_tile), o_tile)
+                value = jnp.dot(mix_buf[source], wo_buf[source, :, cols], preferred_element_type=f32)
+                o_acc[:, cols] = value if j == 0 else o_acc[:, cols] + value
+
+            continue
+        for c in range(chunks):
+
+            @pl.loop(0, chunk // o_tile)
+            def _(n):
+                cols = pl.ds(pl.multiple_of(c * chunk + n * o_tile, o_tile), o_tile)
+                value = jnp.dot(mix_buf[source], wo_buf[source, :, cols], preferred_element_type=f32)
+                o_acc[:, cols] = o_acc[:, cols] + value
+                for r in range(n_head):
+                    o_send[r, :, cols] = o_acc[r * rows : (r + 1) * rows, cols]
+
+            cols = pl.ds(c * chunk, chunk)
+            for r in range(n_head - 1):
+                copy = to(
+                    "head", head_to[r], o_send.at[head_to[r], :, cols], o_recv.at[r, :, cols],
+                    os_sem.at[c * n_head + r], or_sem.at[c * n_head + r],
+                )
+                copy.start()
+                o_copies.append(copy)
+    for c in range(chunks):
+        cols = slice(c * chunk, (c + 1) * chunk)
+        for r in range(n_head - 1):
+            o_copies[c * (n_head - 1) + r].wait_recv()
+        total = o_send[hd, :, cols]
+        for r in range(n_head - 1):
+            total = total + o_recv[r, :, cols]
+        out[:, cols] = total.astype(bf16)
+    for copy in hid_copies + rs_copies + ag_copies + st_copies + ra_copies + mx_copies + o_copies:
+        copy.wait_send()
+
+
+def fused(n_seq, n_head, hidden, norm_gain, w_query, w_key, w_value, w_out, lengths, key_cache, value_cache):
+    rows, feat = hidden.shape
+    batch, kv, block, size = key_cache.shape
+    heads = w_query.shape[1] // size
+    own = heads // n_seq
+    width = own * size
+    columns = w_out.shape[1]
+    f32, bf16 = jnp.float32, jnp.bfloat16
+    hbm = pl.BlockSpec(memory_space=pl.ANY)
+    vmem = pl.BlockSpec(memory_space=pltpu.VMEM)
+    smem = pl.BlockSpec(memory_space=pltpu.SMEM)
+    dma = pltpu.SemaphoreType.DMA
+    steps = [dma((n_seq,)), dma((n_seq,))]
+    return pl.pallas_call(
+        functools.partial(layer_kernel, n_seq, n_head),
+        out_shape=jax.ShapeDtypeStruct((rows, columns), bf16),
+        in_specs=[hbm, vmem, smem] + [hbm] * 6,
+        out_specs=vmem,
+        scratch_shapes=[
+            pltpu.VMEM((n_head, rows, feat), bf16),
+            pltpu.VMEM((batch, feat), f32),
+            pltpu.VMEM((batch, feat), bf16),
+            pltpu.VMEM((batch, block), jnp.int32),
+            pltpu.VMEM((n_seq, feat, width), bf16),
+            pltpu.VMEM((feat, 2 * kv * size), bf16),
+            pltpu.VMEM((n_seq, width, columns), bf16),
+            pltpu.VMEM(key_cache.shape, bf16),
+            pltpu.VMEM(value_cache.shape, bf16),
+            pltpu.VMEM((n_seq, batch, width + size + 128), f32),
+            pltpu.VMEM((n_seq - 1, batch, width + size + 128), f32),
+            pltpu.VMEM((n_seq, batch, width + size), bf16),
+            pltpu.VMEM((heads * batch, size), f32),
+            pltpu.VMEM((heads * batch, block), f32),
+            pltpu.VMEM((heads * batch, size), f32),
+            pltpu.VMEM((n_seq, batch, 128), f32),
+            pltpu.VMEM((n_seq - 1, own * batch, size), f32),
+            pltpu.VMEM((n_seq, batch, width), bf16),
+            pltpu.VMEM((batch, columns), f32),
+            pltpu.VMEM((n_head, rows, columns), f32),
+            pltpu.VMEM((n_head - 1, rows, columns), f32),
+            dma((5 + 2 * n_seq,)),
+            dma((n_head,)),
+            dma((n_head,)),
+            *steps, *steps, *steps, *steps, *steps,
+            dma((4 * n_head,)),
+            dma((4 * n_head,)),
+        ],
+        compiler_params=pltpu.CompilerParams(
+            collective_id=0, has_side_effects=True, vmem_limit_bytes=60 * 1024 * 1024
+        ),
+    )(hidden, norm_gain.reshape(1, feat), lengths, w_query, w_key, w_value, w_out, key_cache, value_cache)
+
+
+def program(n_seq, n_head, *args):
+    w_query, key_cache = args[2], args[7]
+    batch, kv, block, size = key_cache.shape
+    heads = w_query.shape[1] // size
+    own = max(heads // n_seq, 1)
+    fits = (
+        own * n_seq == heads
+        and (heads // kv) % own == 0
+        and 2 * kv == n_seq
+        and size == 128
+        and block == 128
+        and heads <= 64
+        and batch % 8 == 0
+    )
+    return fused(n_seq, n_head, *args) if fits else local(*args)
+
+
 def solution(mesh):
     return jax.shard_map(
-        local,
+        functools.partial(program, mesh.shape["seq"], mesh.shape["head"]),
         mesh=mesh,
         in_specs=(
             P(("parts", "head"), "seq"),

time: 133 us -> 54.2 us (0.41); the launches traced: 131 us -> 54 us
  blocking collectives: 65.9 us -> 0 us
  Pallas kernels: 0 us -> 52.5 us
  matrix products: 21.3 us -> 0 us
  waiting for transfers between devices: 18.1 us -> 0 us
  between operations: 14.3 us -> 0.01 us
  local copies, waits for them, and re-layouts: 6.41 us -> 1.42 us
  other arithmetic: 4.09 us -> 0 us
  starting transfers between devices: 1.34 us -> 0 us
    pallas_call x0 -> x1, Pallas kernels: none -> 52.5 us  [fused(): pl.pallas_call(functools.partial(layer_kernel, n_seq, n_head), out_shape=...]
    all_gather x3 -> x0, blocking collectives: 35 us -> none  [the longest x2 27.8 us: joined(): pieces = jax.tree.map(lambda part: lax.all_gather(part, axis), value)]
    dot_general x7 -> x0, matrix products: 21.3 us -> none  [the longest x1 9.76 us: local(): query_part = jnp.dot(scaled, w_query, preferred_element_type=jnp.float32)]
    psum x1 -> x0, blocking collectives: 21.2 us -> none  [local(): norm_total = lax.psum(square_local, 'seq')]
    psum x1 -> x0, waiting for transfers between devices: 15.1 us -> none  [local(): lax.psum((query_part, key_part, value_part), 'seq')]
    unnamed x1 -> x0, blocking collectives: 9.65 us -> none
    all_gather x1 -> x0, waiting for transfers between devices: 2.93 us -> none  [joined(): pieces = jax.tree.map(lambda part: lax.all_gather(part, axis), value)]
    convert_element_type x3 -> x0, other arithmetic: 1.51 us -> none  [the longest x1 1.06 us: local(): queries = (query_sum * inverse_rms * query_factor).astype(jnp.bfloat16)]
  transfers between devices with their start and end apart: 3 -> 0, of which waited for: 2 -> 0; matrix products, arithmetic and copies ran while one was open for 2% -> 0% of each run, Pallas kernels for 0% -> 0%
where the time goes in v1:
time: 54.2 us; the launch traced here: 54 us
  Pallas kernels  52.5 us (97%)
  local copies, waits for them, and re-layouts  1.42 us (3%)
    pallas_call x1, Pallas kernels, fused(): pl.pallas_call(functools.partial(layer_kernel, n_seq, n_head), out_shape=...  52.5 us
    unnamed x1, local copies, waits for them, and re-layouts  1.42 us

profile of v1, /device:TPU:0, one launch (start us, length us, event | category | flops | bytes accessed | tf_op | source)
XLA Modules:
  0.0 54.0 jit_solution(7038178271739921539)
XLA Ops:
  0.0 52.5 %shard_map.91 = bf16[6,3072]{1,0:T(8,128)(2,1)} custom-call(bf16[6,3072]{1,0:T(8,128)(2,1)} %hid.1, f32[1,3072]{1,0:T(1,128)} %bitcast.1, s32[24]{0:T(128)} %lens.1, bf16[3072,3072]{1,0:T(8,128)(2,1)} %wq.1, bf16[3072,256]{1,0:T(8,128)(2,1)} %wk.1, bf16[3072,256]{1,0:T(8,128)(2,1)} %wv.1, bf16[3072,3072]{1,0:T(8,128)(2,1)} %wo.1, ...), custom_call_target="tpu_custom_call" | custom-call | tf_op jit(solution)/shard_map/pallas_call | solution.py:368
  52.5 1.4 %copy.11 = bf16[6,3072]{1,0:T(8,128)(2,1)} copy(bf16[6,3072]{1,0:T(8,128)(2,1)} %shard_map.91) | data formatting | bytes 73728

commit v2 on v1

--- a/solution.py
+++ b/solution.py
@@ -97,8 +97,8 @@
 def layer_kernel(
     n_seq, n_head, hid, gain, lens, wq, wk, wv, wo, kc, vc, out,
     hid_buf, x_scr, xs_scr, len_scr, wq_buf, wkv_buf, wo_buf, kc_buf, vc_buf,
-    part, rs_buf, ag_buf, q_scr, sc_scr, acc_scr, st_buf, ra_buf, mix_buf, o_acc, o_send, o_recv,
-    load_sem, hid_send, hid_recv, rs_send, rs_recv, ag_send, ag_recv,
+    part, rs_buf, sq_buf, ag_buf, nk_buf, q_scr, sc_scr, acc_scr, st_buf, acc_send, ra_buf, mix_buf, o_acc, o_own, o_send, o_recv,
+    load_sem, hid_send, hid_recv, rs_send, rs_recv, sq_send, sq_recv, ag_send, ag_recv, nk_send, nk_recv,
     st_send, st_recv, ra_send, ra_recv, mx_send, mx_recv, os_sem, or_sem,
 ):
     f32, bf16 = jnp.float32, jnp.bfloat16
@@ -109,7 +109,6 @@
     group = heads // kv
     own = heads // n_seq
     width = own * size
-    tile = 256 if width % 256 == 0 else size
     kv_cols = kv * size
 
     def load(index, source, target):
@@ -128,6 +127,11 @@
     head_to = [lax.rem(hd + j + 1, n_head) for j in range(n_head)]
 
     own_hidden = load(0, hid, hid_buf.at[hd])
+    barrier = pltpu.get_barrier_semaphore()
+    for j in range(n_head - 1):
+        pl.semaphore_signal(barrier, inc=1, device_id={"head": head_to[j]}, device_id_type=MESH)
+    for j in range(n_seq - 1):
+        pl.semaphore_signal(barrier, inc=1, device_id={"seq": seq_to[j]}, device_id_type=MESH)
     key_load = load(1, wk, wkv_buf.at[:, pl.ds(0, kv_cols)])
     value_load = load(2, wv, wkv_buf.at[:, pl.ds(kv_cols, kv_cols)])
     q_loads = [
@@ -141,28 +145,29 @@
         load(base + 2 + j, wo.at[pl.ds(j * width, width)], wo_buf.at[j]) for j in range(n_seq)
     ]
 
-    barrier = pltpu.get_barrier_semaphore()
-    for j in range(n_head - 1):
-        pl.semaphore_signal(barrier, inc=1, device_id={"head": head_to[j]}, device_id_type=MESH)
-    for j in range(n_seq - 1):
-        pl.semaphore_signal(barrier, inc=1, device_id={"seq": seq_to[j]}, device_id_type=MESH)
+    own_hidden.wait()
     pl.semaphore_wait(barrier, n_head + n_seq - 2)
 
     hid_copies = [
-        to("head", head_to[j], hid, hid_buf.at[hd], hid_send.at[j], hid_recv.at[j])
+        to("head", head_to[j], hid_buf.at[hd], hid_buf.at[hd], hid_send.at[j], hid_recv.at[j])
         for j in range(n_head - 1)
     ]
     for copy in hid_copies:
         copy.start()
     for b in range(batch):
         len_scr[b : b + 1, :] = jnp.full((1, block), lens[b], jnp.int32)
-    own_hidden.wait()
     for copy in hid_copies:
         copy.wait_recv()
     for j in range(n_head):
         x_scr[j * rows : (j + 1) * rows, :] = hid_buf[j].astype(f32)
     widened = x_scr[...]
     square = jnp.sum(widened * widened, axis=1, keepdims=True)
+    sq_buf[n_seq - 1] = jnp.broadcast_to(square, (batch, 128))
+    sq_copies = []
+    for j in range(n_seq - 1):
+        copy = to("seq", seq_to[j], sq_buf.at[n_seq - 1], sq_buf.at[j], sq_send.at[j], sq_recv.at[j])
+        copy.start()
+        sq_copies.append(copy)
     xs_scr[...] = (widened * gain[...]).astype(bf16)
 
     key_load.wait()
@@ -171,16 +176,11 @@
     for j in range(n_seq):
         q_loads[j].wait()
 
-        @pl.loop(0, width // tile)
-        def _(n):
-            cols = pl.ds(pl.multiple_of(n * tile, tile), tile)
-            part[j, :, cols] = jnp.dot(xs_scr[...], wq_buf[j, :, cols], preferred_element_type=f32)
-
+        part[j, :, :width] = jnp.dot(xs_scr[...], wq_buf[j], preferred_element_type=f32)
         kv_at = pl.ds(pl.multiple_of(seq_to[j] * size, size), size)
-        part[j, :, width : width + size] = jnp.dot(
+        part[j, :, width:] = jnp.dot(
             xs_scr[...], wkv_buf[:, kv_at], preferred_element_type=f32
         )
-        part[j, :, width + size :] = jnp.broadcast_to(square, (batch, 128))
         if j < n_seq - 1:
             copy = to("seq", seq_to[j], part.at[j], rs_buf.at[j], rs_send.at[j], rs_recv.at[j])
             copy.start()
@@ -195,16 +195,26 @@
             total = total + rs_buf[j, :, cols]
         return total
 
-    mean_square = summed(slice(width + size, width + size + 128)) / (feat * n_seq)
+    for copy in sq_copies:
+        copy.wait_recv()
+    square_sum = sq_buf[0]
+    for j in range(1, n_seq):
+        square_sum = square_sum + sq_buf[j]
+    mean_square = square_sum / (feat * n_seq)
     inverse_rms = lax.rsqrt(mean_square + EPSILON)[:, :1]
     factor = float(size) ** (-0.5)
-    ag_buf[seq, :, :width] = (summed(slice(0, width)) * inverse_rms * factor).astype(bf16)
-    ag_buf[seq, :, width:] = (summed(slice(width, width + size)) * inverse_rms).astype(bf16)
+    ag_buf[seq] = (summed(slice(0, width)) * inverse_rms * factor).astype(bf16)
     ag_copies = []
     for j in range(n_seq - 1):
         copy = to("seq", seq_to[j], ag_buf.at[seq], ag_buf.at[seq], ag_send.at[j], ag_recv.at[j])
         copy.start()
         ag_copies.append(copy)
+    nk_buf[seq] = (summed(slice(width, width + size)) * inverse_rms).astype(bf16)
+    nk_copies = []
+    for j in range(n_seq - 1):
+        copy = to("seq", seq_to[j], nk_buf.at[seq], nk_buf.at[seq], nk_send.at[j], nk_recv.at[j])
+        copy.start()
+        nk_copies.append(copy)
     kc_load.wait()
     vc_load.wait()
     for copy in ag_copies:
@@ -259,13 +269,16 @@
     part_rows = own * batch
     for j in range(n_seq - 1):
         at = pl.ds(pl.multiple_of(seq_to[j] * part_rows, part_rows), part_rows)
-        copy = to("seq", seq_to[j], acc_scr.at[at], ra_buf.at[j], ra_send.at[j], ra_recv.at[j])
+        acc_send[j] = acc_scr[at, :].astype(bf16)
+        copy = to("seq", seq_to[j], acc_send.at[j], ra_buf.at[j], ra_send.at[j], ra_recv.at[j])
         copy.start()
         ra_copies.append(copy)
 
     kv_head = (seq * own) // group
-    new_key = ag_buf[kv_head, :, width:].astype(f32)
-    new_value = ag_buf[kv + kv_head, :, width:].astype(f32)
+    for copy in nk_copies:
+        copy.wait_recv()
+    new_key = nk_buf[kv_head].astype(f32)
+    new_value = nk_buf[kv + kv_head].astype(f32)
     own_at = pl.multiple_of(seq * part_rows, part_rows)
     self_score = jnp.zeros((batch, 128), f32)
     for i in range(own):
@@ -293,7 +306,7 @@
         mixed = own_weight[:, i : i + 1] * new_value
         mixed += factors[n_seq - 1][:, i : i + 1] * acc_scr[pl.ds(own_at + i * batch, batch), :]
         for j in range(n_seq - 1):
-            mixed += factors[j][:, i : i + 1] * ra_buf[j, i * batch : (i + 1) * batch, :]
+            mixed += factors[j][:, i : i + 1] * ra_buf[j, i * batch : (i + 1) * batch, :].astype(f32)
         mix_buf[seq, :, i * size : (i + 1) * size] = mixed.astype(bf16)
     mx_copies = []
     for j in range(n_seq - 1):
@@ -304,52 +317,56 @@
         copy.wait()
 
     columns = wo.shape[1]
-    o_tile = 256 if columns % (4 * 256) == 0 else 128
-    chunks = 4 if columns % (4 * o_tile) == 0 else 1
+    chunks = 4 if columns % 512 == 0 else 1
     chunk = columns // chunks
-    order = [seq] + seq_from[: n_seq - 1]
-    o_copies = []
+
+    def o_copy(c, r):
+        index = c * n_head + r
+        return to(
+            "head", head_to[r], o_send.at[head_to[r], c], o_recv.at[r, c], os_sem.at[index], or_sem.at[index]
+        )
+
+    near = [
+        sorted((o for o in range(n_seq) if o != s), key=lambda o: abs(o - s)) for s in range(n_seq)
+    ]
     for j in range(n_seq):
+        source = seq
         if j > 0:
-            mx_copies[j - 1].wait_recv()
-        source = order[j]
-        if j < n_seq - 1:
-
-            @pl.loop(0, columns // o_tile)
-            def _(n):
-                cols = pl.ds(pl.multiple_of(n * o_tile, o_tile), o_tile)
-                value = jnp.dot(mix_buf[source], wo_buf[source, :, cols], preferred_element_type=f32)
-                o_acc[:, cols] = value if j == 0 else o_acc[:, cols] + value
-
-            continue
-        for c in range(chunks):
-
-            @pl.loop(0, chunk // o_tile)
-            def _(n):
-                cols = pl.ds(pl.multiple_of(c * chunk + n * o_tile, o_tile), o_tile)
-                value = jnp.dot(mix_buf[source], wo_buf[source, :, cols], preferred_element_type=f32)
-                o_acc[:, cols] = o_acc[:, cols] + value
-                for r in range(n_head):
-                    o_send[r, :, cols] = o_acc[r * rows : (r + 1) * rows, cols]
-
-            cols = pl.ds(c * chunk, chunk)
+            source = jnp.int32(0)
+            for s in range(n_seq):
+                source = jnp.where(seq == s, near[s][j - 1], source)
+            slot = lax.rem(seq - source + n_seq - 1, n_seq)
+            to("seq", source, mix_buf.at[source], mix_buf.at[source], mx_send.at[slot], mx_recv.at[slot]).wait_recv()
+        last = j == n_seq - 1
+
+        @pl.loop(0, chunks)
+        def _(c):
+            cols = pl.ds(pl.multiple_of(c * chunk, 128), chunk)
+            value = jnp.dot(mix_buf[source], wo_buf[source, :, cols], preferred_element_type=f32)
+            if j > 0:
+                value = o_acc[:, cols] + value
+            if not last:
+                o_acc[:, cols] = value
+                return
+            for r in range(n_head):
+                o_own[r, :, cols] = value[r * rows : (r + 1) * rows]
+                o_send[r, c] = value[r * rows : (r + 1) * rows].astype(bf16)
             for r in range(n_head - 1):
-                copy = to(
-                    "head", head_to[r], o_send.at[head_to[r], :, cols], o_recv.at[r, :, cols],
-                    os_sem.at[c * n_head + r], or_sem.at[c * n_head + r],
-                )
-                copy.start()
-                o_copies.append(copy)
+                o_copy(c, r).start()
+
     for c in range(chunks):
         cols = slice(c * chunk, (c + 1) * chunk)
         for r in range(n_head - 1):
-            o_copies[c * (n_head - 1) + r].wait_recv()
-        total = o_send[hd, :, cols]
+            o_copy(c, r).wait_recv()
+        total = o_own[hd, :, cols]
         for r in range(n_head - 1):
-            total = total + o_recv[r, :, cols]
+            total = total + o_recv[r, c].astype(f32)
         out[:, cols] = total.astype(bf16)
-    for copy in hid_copies + rs_copies + ag_copies + st_copies + ra_copies + mx_copies + o_copies:
+    for copy in hid_copies + rs_copies + sq_copies + ag_copies + nk_copies + st_copies + ra_copies + mx_copies:
         copy.wait_send()
+    for c in range(chunks):
+        for r in range(n_head - 1):
+            o_copy(c, r).wait_send()
 
 
 def fused(n_seq, n_head, hidden, norm_gain, w_query, w_key, w_value, w_out, lengths, key_cache, value_cache):
@@ -359,6 +376,7 @@
     own = heads // n_seq
     width = own * size
     columns = w_out.shape[1]
+    chunks = 4 if columns % 512 == 0 else 1
     f32, bf16 = jnp.float32, jnp.bfloat16
     hbm = pl.BlockSpec(memory_space=pl.ANY)
     vmem = pl.BlockSpec(memory_space=pltpu.VMEM)
@@ -380,22 +398,26 @@
             pltpu.VMEM((n_seq, width, columns), bf16),
             pltpu.VMEM(key_cache.shape, bf16),
             pltpu.VMEM(value_cache.shape, bf16),
-            pltpu.VMEM((n_seq, batch, width + size + 128), f32),
-            pltpu.VMEM((n_seq - 1, batch, width + size + 128), f32),
-            pltpu.VMEM((n_seq, batch, width + size), bf16),
+            pltpu.VMEM((n_seq, batch, width + size), f32),
+            pltpu.VMEM((n_seq - 1, batch, width + size), f32),
+            pltpu.VMEM((n_seq, batch, 128), f32),
+            pltpu.VMEM((n_seq, batch, width), bf16),
+            pltpu.VMEM((n_seq, batch, size), bf16),
             pltpu.VMEM((heads * batch, size), f32),
             pltpu.VMEM((heads * batch, block), f32),
             pltpu.VMEM((heads * batch, size), f32),
             pltpu.VMEM((n_seq, batch, 128), f32),
-            pltpu.VMEM((n_seq - 1, own * batch, size), f32),
+            pltpu.VMEM((n_seq - 1, own * batch, size), bf16),
+            pltpu.VMEM((n_seq - 1, own * batch, size), bf16),
             pltpu.VMEM((n_seq, batch, width), bf16),
             pltpu.VMEM((batch, columns), f32),
             pltpu.VMEM((n_head, rows, columns), f32),
-            pltpu.VMEM((n_head - 1, rows, columns), f32),
+            pltpu.VMEM((n_head, chunks, rows, columns // chunks), bf16),
+            pltpu.VMEM((n_head - 1, chunks, rows, columns // chunks), bf16),
             dma((5 + 2 * n_seq,)),
             dma((n_head,)),
             dma((n_head,)),
-            *steps, *steps, *steps, *steps, *steps,
+            *steps, *steps, *steps, *steps, *steps, *steps, *steps,
             dma((4 * n_head,)),
             dma((4 * n_head,)),
         ],

time: 54.2 us -> 46.7 us (0.86)
  Pallas kernels: 52.5 us -> 45 us
    pallas_call x1, Pallas kernels: 52.5 us -> 45 us  [fused(): pl.pallas_call(functools.partial(layer_kernel, n_seq, n_head), out_shape=...]
where the time goes in v2:
time: 46.7 us; the launch traced here: 46.5 us
  Pallas kernels  45 us (96%)
  local copies, waits for them, and re-layouts  1.42 us (3%)
    pallas_call x1, Pallas kernels, fused(): pl.pallas_call(functools.partial(layer_kernel, n_seq, n_head), out_shape=...  45 us
    unnamed x1, local copies, waits for them, and re-layouts  1.42 us

profile of v2, /device:TPU:0, one launch (start us, length us, event | category | flops | bytes accessed | tf_op | source)
XLA Modules:
  0.0 46.5 jit_solution(15217607420663401343)
XLA Ops:
  0.0 45.0 %shard_map.91 = bf16[6,3072]{1,0:T(8,128)(2,1)} custom-call(bf16[6,3072]{1,0:T(8,128)(2,1)} %hid.1, f32[1,3072]{1,0:T(1,128)} %bitcast.1, s32[24]{0:T(128)} %lens.1, bf16[3072,3072]{1,0:T(8,128)(2,1)} %wq.1, bf16[3072,256]{1,0:T(8,128)(2,1)} %wk.1, bf16[3072,256]{1,0:T(8,128)(2,1)} %wv.1, bf16[3072,3072]{1,0:T(8,128)(2,1)} %wo.1, ...), custom_call_target="tpu_custom_call" | custom-call | tf_op jit(solution)/shard_map/pallas_call | solution.py:386
  45.0 1.4 %copy.11 = bf16[6,3072]{1,0:T(8,128)(2,1)} copy(bf16[6,3072]{1,0:T(8,128)(2,1)} %shard_map.91) | data formatting | bytes 73728

commit v3 on v2

--- a/solution.py
+++ b/solution.py
@@ -97,8 +97,8 @@
 def layer_kernel(
     n_seq, n_head, hid, gain, lens, wq, wk, wv, wo, kc, vc, out,
     hid_buf, x_scr, xs_scr, len_scr, wq_buf, wkv_buf, wo_buf, kc_buf, vc_buf,
-    part, rs_buf, sq_buf, ag_buf, nk_buf, q_scr, sc_scr, acc_scr, st_buf, acc_send, ra_buf, mix_buf, o_acc, o_own, o_send, o_recv,
-    load_sem, hid_send, hid_recv, rs_send, rs_recv, sq_send, sq_recv, ag_send, ag_recv, nk_send, nk_recv,
+    part, rs_buf, kv_part, kv_buf, sq_buf, ag_buf, nk_buf, q_scr, sc_scr, acc_scr, st_buf, acc_send, ra_buf, mix_buf, o_acc, o_own, o_send, o_recv,
+    load_sem, hid_send, hid_recv, rs_send, rs_recv, kv_send, kv_recv, sq_send, sq_recv, ag_send, ag_recv, nk_send, nk_recv,
     st_send, st_recv, ra_send, ra_recv, mx_send, mx_recv, os_sem, or_sem,
 ):
     f32, bf16 = jnp.float32, jnp.bfloat16
@@ -170,30 +170,26 @@
         sq_copies.append(copy)
     xs_scr[...] = (widened * gain[...]).astype(bf16)
 
-    key_load.wait()
-    value_load.wait()
+    tile = 256 if width % 256 == 0 else size
+    pieces = width // tile
     rs_copies = []
     for j in range(n_seq):
         q_loads[j].wait()
-
-        part[j, :, :width] = jnp.dot(xs_scr[...], wq_buf[j], preferred_element_type=f32)
+        for n in range(pieces):
+            cols = slice(n * tile, (n + 1) * tile)
+            part[j, n] = jnp.dot(xs_scr[...], wq_buf[j, :, cols], preferred_element_type=f32)
+            if j < n_seq - 1:
+                index = j * pieces + n
+                copy = to(
+                    "seq", seq_to[j], part.at[j, n], rs_buf.at[j, n], rs_send.at[index], rs_recv.at[index]
+                )
+                copy.start()
+                rs_copies.append(copy)
+    key_load.wait()
+    value_load.wait()
+    for j in range(n_seq):
         kv_at = pl.ds(pl.multiple_of(seq_to[j] * size, size), size)
-        part[j, :, width:] = jnp.dot(
-            xs_scr[...], wkv_buf[:, kv_at], preferred_element_type=f32
-        )
-        if j < n_seq - 1:
-            copy = to("seq", seq_to[j], part.at[j], rs_buf.at[j], rs_send.at[j], rs_recv.at[j])
-            copy.start()
-            rs_copies.append(copy)
-
-    for copy in rs_copies:
-        copy.wait_recv()
-
-    def summed(cols):
-        total = part[n_seq - 1, :, cols]
-        for j in range(n_seq - 1):
-            total = total + rs_buf[j, :, cols]
-        return total
+        kv_part[j] = jnp.dot(xs_scr[...], wkv_buf[:, kv_at], preferred_element_type=f32)
 
     for copy in sq_copies:
         copy.wait_recv()
@@ -203,68 +199,106 @@
     mean_square = square_sum / (feat * n_seq)
     inverse_rms = lax.rsqrt(mean_square + EPSILON)[:, :1]
     factor = float(size) ** (-0.5)
-    ag_buf[seq] = (summed(slice(0, width)) * inverse_rms * factor).astype(bf16)
+    for n in range(pieces):
+        total = part[n_seq - 1, n]
+        for j in range(n_seq - 1):
+            rs_copies[j * pieces + n].wait_recv()
+            total = total + rs_buf[j, n]
+        ag_buf[seq, :, n * tile : (n + 1) * tile] = (total * inverse_rms * factor).astype(bf16)
     ag_copies = []
     for j in range(n_seq - 1):
         copy = to("seq", seq_to[j], ag_buf.at[seq], ag_buf.at[seq], ag_send.at[j], ag_recv.at[j])
         copy.start()
         ag_copies.append(copy)
-    nk_buf[seq] = (summed(slice(width, width + size)) * inverse_rms).astype(bf16)
-    nk_copies = []
-    for j in range(n_seq - 1):
-        copy = to("seq", seq_to[j], nk_buf.at[seq], nk_buf.at[seq], nk_send.at[j], nk_recv.at[j])
-        copy.start()
-        nk_copies.append(copy)
+    kv_copies = []
+    for j in range(n_seq - 1):
+        copy = to("seq", seq_to[j], kv_part.at[j], kv_buf.at[j], kv_send.at[j], kv_recv.at[j])
+        copy.start()
+        kv_copies.append(copy)
     kc_load.wait()
     vc_load.wait()
-    for copy in ag_copies:
-        copy.wait_recv()
-    for s in range(n_seq):
+    unroll = 6 if batch % 6 == 0 else 1
+    sources = n_seq // kv
+
+    def take_queries(source, remote):
+        if remote:
+            slot = lax.rem(seq - source + n_seq - 1, n_seq)
+            to("seq", source, ag_buf.at[source], ag_buf.at[source], ag_send.at[slot], ag_recv.at[slot]).wait_recv()
         for i in range(own):
-            at = (s * own + i) * batch
-            q_scr[at : at + batch, :] = ag_buf[s, :, i * size : (i + 1) * size].astype(f32)
-
-    unroll = 4 if batch % 4 == 0 else 1
-
-    @pl.loop(0, batch // unroll)
-    def _(step):
-        for u in range(unroll):
-            b = step * unroll + u
-            for k in range(kv):
+            at = pl.multiple_of((source * own + i) * batch, 8)
+            q_scr[pl.ds(at, batch), :] = ag_buf[source, :, i * size : (i + 1) * size].astype(f32)
+
+    def score(k):
+        @pl.loop(0, batch // unroll)
+        def _(step):
+            for u in range(unroll):
+                b = step * unroll + u
                 at = pl.ds(k * group * batch + b, group, stride=batch)
                 sc_scr[at, :] = lax.dot_general(
                     q_scr[at, :].astype(bf16), kc_buf[b, k], (((1,), (1,)), ((), ())),
                     preferred_element_type=f32,
                 )
 
-    lane = lax.broadcasted_iota(jnp.int32, (batch, block), 1)
-    live = lane + seq * block < len_scr[...]
-    stats = jnp.zeros((batch, 128), f32)
-    for h in range(heads):
-        scores = sc_scr[h * batch : (h + 1) * batch, :]
-        top = jnp.max(jnp.where(live, scores, -1e30), axis=1, keepdims=True)
-        shifted = jnp.where(live, scores - top, 0.0)
-        weights = jnp.where(live, jnp.exp(shifted), 0.0).astype(bf16).astype(f32)
-        sc_scr[h * batch : (h + 1) * batch, :] = weights
-        total = jnp.sum(weights, axis=1, keepdims=True)
-        stats = jnp.where(lane == h, top, jnp.where(lane == 64 + h, total, stats))
-    st_buf[n_seq - 1] = stats
-    st_copies = []
-    for j in range(n_seq - 1):
-        copy = to("seq", seq_to[j], st_buf.at[n_seq - 1], st_buf.at[j], st_send.at[j], st_recv.at[j])
-        copy.start()
-        st_copies.append(copy)
-
-    @pl.loop(0, batch // unroll)
-    def _(step):
-        for u in range(unroll):
-            b = step * unroll + u
-            for k in range(kv):
+    def accumulate(k):
+        @pl.loop(0, batch // unroll)
+        def _(step):
+            for u in range(unroll):
+                b = step * unroll + u
                 at = pl.ds(k * group * batch + b, group, stride=batch)
                 acc_scr[at, :] = jnp.dot(
                     sc_scr[at, :].astype(bf16), vc_buf[b, k], preferred_element_type=f32
                 )
 
+    lane = lax.broadcasted_iota(jnp.int32, (batch, block), 1)
+    live = lane + seq * block < len_scr[...]
+
+    def soften(k, stats):
+        for g in range(group):
+            h = k * group + g
+            at = pl.ds(pl.multiple_of(h * batch, 8), batch)
+            scores = sc_scr[at, :]
+            top = jnp.max(jnp.where(live, scores, -1e30), axis=1, keepdims=True)
+            shifted = jnp.where(live, scores - top, 0.0)
+            weights = jnp.where(live, jnp.exp(shifted), 0.0).astype(bf16).astype(f32)
+            sc_scr[at, :] = weights
+            total = jnp.sum(weights, axis=1, keepdims=True)
+            stats = jnp.where(lane == h, top, jnp.where(lane == 64 + h, total, stats))
+        return stats
+
+    kv_head = (seq * own) // group
+    stats = jnp.zeros((batch, 128), f32)
+    take_queries(seq, False)
+    for t in range(1, sources):
+        take_queries(kv_head * sources + lax.rem(seq + t, sources), True)
+    score(kv_head)
+    stats = soften(kv_head, stats)
+    if kv > 1:
+        accumulate(kv_head)
+    others = [lax.rem(kv_head + t, kv) for t in range(1, kv)]
+    for k in others:
+        for t in range(sources):
+            take_queries(k * sources + t, True)
+        score(k)
+        stats = soften(k, stats)
+    st_buf[n_seq - 1] = stats
+    st_copies = []
+    for j in range(n_seq - 1):
+        copy = to("seq", seq_to[j], st_buf.at[n_seq - 1], st_buf.at[j], st_send.at[j], st_recv.at[j])
+        copy.start()
+        st_copies.append(copy)
+    new_part = kv_part[n_seq - 1]
+    for j in range(n_seq - 1):
+        kv_copies[j].wait_recv()
+        new_part = new_part + kv_buf[j]
+    nk_buf[seq] = (new_part * inverse_rms).astype(bf16)
+    nk_copies = []
+    for j in range(n_seq - 1):
+        copy = to("seq", seq_to[j], nk_buf.at[seq], nk_buf.at[seq], nk_send.at[j], nk_recv.at[j])
+        copy.start()
+        nk_copies.append(copy)
+    for k in others if kv > 1 else [kv_head]:
+        accumulate(k)
+
     ra_copies = []
     part_rows = own * batch
     for j in range(n_seq - 1):
@@ -274,7 +308,6 @@
         copy.start()
         ra_copies.append(copy)
 
-    kv_head = (seq * own) // group
     for copy in nk_copies:
         copy.wait_recv()
     new_key = nk_buf[kv_head].astype(f32)
@@ -362,7 +395,7 @@
         for r in range(n_head - 1):
             total = total + o_recv[r, c].astype(f32)
         out[:, cols] = total.astype(bf16)
-    for copy in hid_copies + rs_copies + sq_copies + ag_copies + nk_copies + st_copies + ra_copies + mx_copies:
+    for copy in hid_copies + rs_copies + kv_copies + sq_copies + ag_copies + nk_copies + st_copies + ra_copies + mx_copies:
         copy.wait_send()
     for c in range(chunks):
         for r in range(n_head - 1):
@@ -375,6 +408,7 @@
     heads = w_query.shape[1] // size
     own = heads // n_seq
     width = own * size
+    tile = 256 if width % 256 == 0 else size
     columns = w_out.shape[1]
     chunks = 4 if columns % 512 == 0 else 1
     f32, bf16 = jnp.float32, jnp.bfloat16
@@ -398,8 +432,10 @@
             pltpu.VMEM((n_seq, width, columns), bf16),
             pltpu.VMEM(key_cache.shape, bf16),
             pltpu.VMEM(value_cache.shape, bf16),
-            pltpu.VMEM((n_seq, batch, width + size), f32),
-            pltpu.VMEM((n_seq - 1, batch, width + size), f32),
+            pltpu.VMEM((n_seq, width // tile, batch, tile), f32),
+            pltpu.VMEM((n_seq - 1, width // tile, batch, tile), f32),
+            pltpu.VMEM((n_seq, batch, size), f32),
+            pltpu.VMEM((n_seq - 1, batch, size), f32),
             pltpu.VMEM((n_seq, batch, 128), f32),
             pltpu.VMEM((n_seq, batch, width), bf16),
             pltpu.VMEM((n_seq, batch, size), bf16),
@@ -417,6 +453,8 @@
             dma((5 + 2 * n_seq,)),
             dma((n_head,)),
             dma((n_head,)),
+            dma((n_seq * width // tile,)),
+            dma((n_seq * width // tile,)),
             *steps, *steps, *steps, *steps, *steps, *steps, *steps,
             dma((4 * n_head,)),
             dma((4 * n_head,)),

time: 46.7 us -> 47.1 us (level)
  Pallas kernels: 45 us -> 45.5 us
where the time goes in v3:
time: 47.1 us; the launch traced here: 46.9 us
  Pallas kernels  45.5 us (97%)
  local copies, waits for them, and re-layouts  1.42 us (3%)
    pallas_call x1, Pallas kernels, fused(): pl.pallas_call(functools.partial(layer_kernel, n_seq, n_head), out_shape=...  45.5 us
    unnamed x1, local copies, waits for them, and re-layouts  1.42 us

profile of v3, /device:TPU:0, one launch (start us, length us, event | category | flops | bytes accessed | tf_op | source)
XLA Modules:
  0.0 46.9 jit_solution(15845170523947464835)
XLA Ops:
  0.0 45.5 %shard_map.91 = bf16[6,3072]{1,0:T(8,128)(2,1)} custom-call(bf16[6,3072]{1,0:T(8,128)(2,1)} %hid.1, f32[1,3072]{1,0:T(1,128)} %bitcast.1, s32[24]{0:T(128)} %lens.1, bf16[3072,3072]{1,0:T(8,128)(2,1)} %wq.1, bf16[3072,256]{1,0:T(8,128)(2,1)} %wk.1, bf16[3072,256]{1,0:T(8,128)(2,1)} %wv.1, bf16[3072,3072]{1,0:T(8,128)(2,1)} %wo.1, ...), custom_call_target="tpu_custom_call" | custom-call | tf_op jit(solution)/shard_map/pallas_call | solution.py:420
  45.5 1.4 %copy.11 = bf16[6,3072]{1,0:T(8,128)(2,1)} copy(bf16[6,3072]{1,0:T(8,128)(2,1)} %shard_map.91) | data formatting | bytes 73728

commit v4 on v3

--- a/solution.py
+++ b/solution.py
@@ -122,8 +122,20 @@
             device_id={axis: index}, device_id_type=MESH,
         )
 
-    seq_to = [lax.rem(seq + j + 1, n_seq) for j in range(n_seq)]
-    seq_from = [lax.rem(seq + n_seq - j - 1, n_seq) for j in range(n_seq)]
+    near = [
+        sorted((o for o in range(n_seq) if o != s), key=lambda o: abs(o - s)) for s in range(n_seq)
+    ]
+
+    def nearest(j):
+        device = jnp.int32(0)
+        for s in range(n_seq):
+            device = jnp.where(seq == s, near[s][j], device)
+        return device
+
+    seq_to = [nearest(n_seq - 2 - j) for j in range(n_seq - 1)] + [seq]
+    slots = [lax.rem(seq_to[j] - seq + n_seq - 1, n_seq) for j in range(n_seq - 1)]
+    tile = 256 if width % 256 == 0 else size
+    pieces = width // tile
     head_to = [lax.rem(hd + j + 1, n_head) for j in range(n_head)]
 
     own_hidden = load(0, hid, hid_buf.at[hd])
@@ -132,13 +144,17 @@
         pl.semaphore_signal(barrier, inc=1, device_id={"head": head_to[j]}, device_id_type=MESH)
     for j in range(n_seq - 1):
         pl.semaphore_signal(barrier, inc=1, device_id={"seq": seq_to[j]}, device_id_type=MESH)
+    q_loads = [
+        load(
+            3 + n * n_seq + j,
+            wq.at[:, pl.ds(pl.multiple_of(seq_to[j] * width + n * tile, tile), tile)],
+            wq_buf.at[n * n_seq + j],
+        )
+        for n in range(pieces) for j in range(n_seq)
+    ]
     key_load = load(1, wk, wkv_buf.at[:, pl.ds(0, kv_cols)])
     value_load = load(2, wv, wkv_buf.at[:, pl.ds(kv_cols, kv_cols)])
-    q_loads = [
-        load(3 + j, wq.at[:, pl.ds(pl.multiple_of(seq_to[j] * width, width), width)], wq_buf.at[j])
-        for j in range(n_seq)
-    ]
-    base = 3 + n_seq
+    base = 3 + n_seq * pieces
     kc_load = load(base, kc, kc_buf)
     vc_load = load(base + 1, vc, vc_buf)
     o_loads = [
@@ -165,23 +181,20 @@
     sq_buf[n_seq - 1] = jnp.broadcast_to(square, (batch, 128))
     sq_copies = []
     for j in range(n_seq - 1):
-        copy = to("seq", seq_to[j], sq_buf.at[n_seq - 1], sq_buf.at[j], sq_send.at[j], sq_recv.at[j])
+        copy = to("seq", seq_to[j], sq_buf.at[n_seq - 1], sq_buf.at[slots[j]], sq_send.at[j], sq_recv.at[slots[j]])
         copy.start()
         sq_copies.append(copy)
     xs_scr[...] = (widened * gain[...]).astype(bf16)
 
-    tile = 256 if width % 256 == 0 else size
-    pieces = width // tile
     rs_copies = []
-    for j in range(n_seq):
-        q_loads[j].wait()
-        for n in range(pieces):
-            cols = slice(n * tile, (n + 1) * tile)
-            part[j, n] = jnp.dot(xs_scr[...], wq_buf[j, :, cols], preferred_element_type=f32)
+    for n in range(pieces):
+        for j in range(n_seq):
+            q_loads[n * n_seq + j].wait()
+            part[j, n] = jnp.dot(xs_scr[...], wq_buf[n * n_seq + j], preferred_element_type=f32)
             if j < n_seq - 1:
-                index = j * pieces + n
                 copy = to(
-                    "seq", seq_to[j], part.at[j, n], rs_buf.at[j, n], rs_send.at[index], rs_recv.at[index]
+                    "seq", seq_to[j], part.at[j, n], rs_buf.at[slots[j], n],
+                    rs_send.at[j * pieces + n], rs_recv.at[slots[j] * pieces + n],
                 )
                 copy.start()
                 rs_copies.append(copy)
@@ -199,20 +212,24 @@
     mean_square = square_sum / (feat * n_seq)
     inverse_rms = lax.rsqrt(mean_square + EPSILON)[:, :1]
     factor = float(size) ** (-0.5)
+    ag_copies = []
     for n in range(pieces):
+        for j in range(n_seq - 1):
+            rs_copies[n * (n_seq - 1) + j].wait_recv()
         total = part[n_seq - 1, n]
         for j in range(n_seq - 1):
-            rs_copies[j * pieces + n].wait_recv()
             total = total + rs_buf[j, n]
-        ag_buf[seq, :, n * tile : (n + 1) * tile] = (total * inverse_rms * factor).astype(bf16)
-    ag_copies = []
-    for j in range(n_seq - 1):
-        copy = to("seq", seq_to[j], ag_buf.at[seq], ag_buf.at[seq], ag_send.at[j], ag_recv.at[j])
-        copy.start()
-        ag_copies.append(copy)
+        ag_buf[seq, n] = (total * inverse_rms * factor).astype(bf16)
+        for j in range(n_seq - 1):
+            copy = to(
+                "seq", seq_to[j], ag_buf.at[seq, n], ag_buf.at[seq, n],
+                ag_send.at[j * pieces + n], ag_recv.at[slots[j] * pieces + n],
+            )
+            copy.start()
+            ag_copies.append(copy)
     kv_copies = []
     for j in range(n_seq - 1):
-        copy = to("seq", seq_to[j], kv_part.at[j], kv_buf.at[j], kv_send.at[j], kv_recv.at[j])
+        copy = to("seq", seq_to[j], kv_part.at[j], kv_buf.at[slots[j]], kv_send.at[j], kv_recv.at[slots[j]])
         copy.start()
         kv_copies.append(copy)
     kc_load.wait()
@@ -223,10 +240,15 @@
     def take_queries(source, remote):
         if remote:
             slot = lax.rem(seq - source + n_seq - 1, n_seq)
-            to("seq", source, ag_buf.at[source], ag_buf.at[source], ag_send.at[slot], ag_recv.at[slot]).wait_recv()
+            for n in range(pieces):
+                index = slot * pieces + n
+                to(
+                    "seq", source, ag_buf.at[source, n], ag_buf.at[source, n], ag_send.at[index], ag_recv.at[index]
+                ).wait_recv()
         for i in range(own):
             at = pl.multiple_of((source * own + i) * batch, 8)
-            q_scr[pl.ds(at, batch), :] = ag_buf[source, :, i * size : (i + 1) * size].astype(f32)
+            n, first = divmod(i * size, tile)
+            q_scr[pl.ds(at, batch), :] = ag_buf[source, n, :, first : first + size].astype(f32)
 
     def score(k):
         @pl.loop(0, batch // unroll)
@@ -283,17 +305,18 @@
     st_buf[n_seq - 1] = stats
     st_copies = []
     for j in range(n_seq - 1):
-        copy = to("seq", seq_to[j], st_buf.at[n_seq - 1], st_buf.at[j], st_send.at[j], st_recv.at[j])
+        copy = to("seq", seq_to[j], st_buf.at[n_seq - 1], st_buf.at[slots[j]], st_send.at[j], st_recv.at[slots[j]])
         copy.start()
         st_copies.append(copy)
     new_part = kv_part[n_seq - 1]
-    for j in range(n_seq - 1):
-        kv_copies[j].wait_recv()
+    for copy in kv_copies:
+        copy.wait_recv()
+    for j in range(n_seq - 1):
         new_part = new_part + kv_buf[j]
     nk_buf[seq] = (new_part * inverse_rms).astype(bf16)
     nk_copies = []
     for j in range(n_seq - 1):
-        copy = to("seq", seq_to[j], nk_buf.at[seq], nk_buf.at[seq], nk_send.at[j], nk_recv.at[j])
+        copy = to("seq", seq_to[j], nk_buf.at[seq], nk_buf.at[seq], nk_send.at[j], nk_recv.at[slots[j]])
         copy.start()
         nk_copies.append(copy)
     for k in others if kv > 1 else [kv_head]:
@@ -304,9 +327,17 @@
     for j in range(n_seq - 1):
         at = pl.ds(pl.multiple_of(seq_to[j] * part_rows, part_rows), part_rows)
         acc_send[j] = acc_scr[at, :].astype(bf16)
-        copy = to("seq", seq_to[j], acc_send.at[j], ra_buf.at[j], ra_send.at[j], ra_recv.at[j])
-        copy.start()
-        ra_copies.append(copy)
+    piece_heads = tile // size
+    piece_rows = piece_heads * batch
+    for n in range(pieces):
+        for j in range(n_seq - 1):
+            copy = to(
+                "seq", seq_to[j], acc_send.at[j, pl.ds(n * piece_rows, piece_rows)],
+                ra_buf.at[slots[j], pl.ds(n * piece_rows, piece_rows)],
+                ra_send.at[j * pieces + n], ra_recv.at[slots[j] * pieces + n],
+            )
+            copy.start()
+            ra_copies.append(copy)
 
     for copy in nk_copies:
         copy.wait_recv()
@@ -333,25 +364,33 @@
         denominator = denominator + f * d
     own_weight = own_weight / denominator
     factors = [f / denominator for f in factors]
-    for copy in ra_copies:
-        copy.wait_recv()
-    for i in range(own):
-        mixed = own_weight[:, i : i + 1] * new_value
-        mixed += factors[n_seq - 1][:, i : i + 1] * acc_scr[pl.ds(own_at + i * batch, batch), :]
+    mx_copies = []
+    for n in range(pieces):
         for j in range(n_seq - 1):
-            mixed += factors[j][:, i : i + 1] * ra_buf[j, i * batch : (i + 1) * batch, :].astype(f32)
-        mix_buf[seq, :, i * size : (i + 1) * size] = mixed.astype(bf16)
-    mx_copies = []
-    for j in range(n_seq - 1):
-        copy = to("seq", seq_to[j], mix_buf.at[seq], mix_buf.at[seq], mx_send.at[j], mx_recv.at[j])
-        copy.start()
-        mx_copies.append(copy)
+            ra_copies[n * (n_seq - 1) + j].wait_recv()
+        for p in range(piece_heads):
+            i = n * piece_heads + p
+            mixed = own_weight[:, i : i + 1] * new_value
+            mixed += factors[n_seq - 1][:, i : i + 1] * acc_scr[pl.ds(own_at + i * batch, batch), :]
+            for j in range(n_seq - 1):
+                mixed += factors[j][:, i : i + 1] * ra_buf[j, i * batch : (i + 1) * batch, :].astype(f32)
+            mix_buf[seq, n, :, p * size : (p + 1) * size] = mixed.astype(bf16)
+        for j in range(n_seq - 1):
+            copy = to(
+                "seq", seq_to[j], mix_buf.at[seq, n], mix_buf.at[seq, n],
+                mx_send.at[j * pieces + n], mx_recv.at[slots[j] * pieces + n],
+            )
+            copy.start()
+            mx_copies.append(copy)
     for copy in o_loads:
         copy.wait()
 
     columns = wo.shape[1]
     chunks = 4 if columns % 512 == 0 else 1
     chunk = columns // chunks
+
+    def mix_of(source):
+        return jnp.concatenate([mix_buf[source, n] for n in range(pieces)], axis=1)
 
     def o_copy(c, r):
         index = c * n_head + r
@@ -359,23 +398,22 @@
             "head", head_to[r], o_send.at[head_to[r], c], o_recv.at[r, c], os_sem.at[index], or_sem.at[index]
         )
 
-    near = [
-        sorted((o for o in range(n_seq) if o != s), key=lambda o: abs(o - s)) for s in range(n_seq)
-    ]
     for j in range(n_seq):
         source = seq
         if j > 0:
-            source = jnp.int32(0)
-            for s in range(n_seq):
-                source = jnp.where(seq == s, near[s][j - 1], source)
+            source = nearest(j - 1)
             slot = lax.rem(seq - source + n_seq - 1, n_seq)
-            to("seq", source, mix_buf.at[source], mix_buf.at[source], mx_send.at[slot], mx_recv.at[slot]).wait_recv()
+            for n in range(pieces):
+                index = slot * pieces + n
+                to(
+                    "seq", source, mix_buf.at[source, n], mix_buf.at[source, n], mx_send.at[index], mx_recv.at[index]
+                ).wait_recv()
         last = j == n_seq - 1
 
         @pl.loop(0, chunks)
         def _(c):
             cols = pl.ds(pl.multiple_of(c * chunk, 128), chunk)
-            value = jnp.dot(mix_buf[source], wo_buf[source, :, cols], preferred_element_type=f32)
+            value = jnp.dot(mix_of(source), wo_buf[source, :, cols], preferred_element_type=f32)
             if j > 0:
                 value = o_acc[:, cols] + value
             if not last:
@@ -417,6 +455,7 @@
     smem = pl.BlockSpec(memory_space=pltpu.SMEM)
     dma = pltpu.SemaphoreType.DMA
     steps = [dma((n_seq,)), dma((n_seq,))]
+    many = [dma((n_seq * width // tile,)), dma((n_seq * width // tile,))]
     return pl.pallas_call(
         functools.partial(layer_kernel, n_seq, n_head),
         out_shape=jax.ShapeDtypeStruct((rows, columns), bf16),
@@ -427,7 +466,7 @@
             pltpu.VMEM((batch, feat), f32),
             pltpu.VMEM((batch, feat), bf16),
             pltpu.VMEM((batch, block), jnp.int32),
-            pltpu.VMEM((n_seq, feat, width), bf16),
+            pltpu.VMEM((n_seq * width // tile, feat, tile), bf16),
             pltpu.VMEM((feat, 2 * kv * size), bf16),
             pltpu.VMEM((n_seq, width, columns), bf16),
             pltpu.VMEM(key_cache.shape, bf16),
@@ -437,7 +476,7 @@
             pltpu.VMEM((n_seq, batch, size), f32),
             pltpu.VMEM((n_seq - 1, batch, size), f32),
             pltpu.VMEM((n_seq, batch, 128), f32),
-            pltpu.VMEM((n_seq, batch, width), bf16),
+            pltpu.VMEM((n_seq, width // tile, batch, tile), bf16),
             pltpu.VMEM((n_seq, batch, size), bf16),
             pltpu.VMEM((heads * batch, size), f32),
             pltpu.VMEM((heads * batch, block), f32),
@@ -445,17 +484,15 @@
             pltpu.VMEM((n_seq, batch, 128), f32),
             pltpu.VMEM((n_seq - 1, own * batch, size), bf16),
             pltpu.VMEM((n_seq - 1, own * batch, size), bf16),
-            pltpu.VMEM((n_seq, batch, width), bf16),
+            pltpu.VMEM((n_seq, width // tile, batch, tile), bf16),
             pltpu.VMEM((batch, columns), f32),
             pltpu.VMEM((n_head, rows, columns), f32),
             pltpu.VMEM((n_head, chunks, rows, columns // chunks), bf16),
             pltpu.VMEM((n_head - 1, chunks, rows, columns // chunks), bf16),
-            dma((5 + 2 * n_seq,)),
+            dma((5 + n_seq + n_seq * width // tile,)),
             dma((n_head,)),
             dma((n_head,)),
-            dma((n_seq * width // tile,)),
-            dma((n_seq * width // tile,)),
-            *steps, *steps, *steps, *steps, *steps, *steps, *steps,
+            *many, *steps, *steps, *many, *steps, *steps, *many, *many,
             dma((4 * n_head,)),
             dma((4 * n_head,)),
         ],

time: 47.1 us -> 44.9 us (0.953)
  Pallas kernels: 45.5 us -> 43.2 us
    pallas_call x1, Pallas kernels: 45.5 us -> 43.2 us  [fused(): pl.pallas_call(functools.partial(layer_kernel, n_seq, n_head), out_shape=...]
where the time goes in v4:
time: 44.9 us; the launch traced here: 44.7 us
  Pallas kernels  43.2 us (96%)
  local copies, waits for them, and re-layouts  1.42 us (3%)
    pallas_call x1, Pallas kernels, fused(): pl.pallas_call(functools.partial(layer_kernel, n_seq, n_head), out_shape=...  43.2 us
    unnamed x1, local copies, waits for them, and re-layouts  1.42 us

profile of v4, /device:TPU:0, one launch (start us, length us, event | category | flops | bytes accessed | tf_op | source)
XLA Modules:
  0.0 44.7 jit_solution(11569824227558027762)
XLA Ops:
  0.0 43.2 %shard_map.91 = bf16[6,3072]{1,0:T(8,128)(2,1)} custom-call(bf16[6,3072]{1,0:T(8,128)(2,1)} %hid.1, f32[1,3072]{1,0:T(1,128)} %bitcast.1, s32[24]{0:T(128)} %lens.1, bf16[3072,3072]{1,0:T(8,128)(2,1)} %wq.1, bf16[3072,256]{1,0:T(8,128)(2,1)} %wk.1, bf16[3072,256]{1,0:T(8,128)(2,1)} %wv.1, bf16[3072,3072]{1,0:T(8,128)(2,1)} %wo.1, ...), custom_call_target="tpu_custom_call" | custom-call | tf_op jit(solution)/shard_map/pallas_call | solution.py:459
  43.2 1.4 %copy.11 = bf16[6,3072]{1,0:T(8,128)(2,1)} copy(bf16[6,3072]{1,0:T(8,128)(2,1)} %shard_map.91) | data formatting | bytes 73728

commit v5 on v4

--- a/solution.py
+++ b/solution.py
@@ -198,12 +198,6 @@
                 )
                 copy.start()
                 rs_copies.append(copy)
-    key_load.wait()
-    value_load.wait()
-    for j in range(n_seq):
-        kv_at = pl.ds(pl.multiple_of(seq_to[j] * size, size), size)
-        kv_part[j] = jnp.dot(xs_scr[...], wkv_buf[:, kv_at], preferred_element_type=f32)
-
     for copy in sq_copies:
         copy.wait_recv()
     square_sum = sq_buf[0]
@@ -227,6 +221,11 @@
             )
             copy.start()
             ag_copies.append(copy)
+    key_load.wait()
+    value_load.wait()
+    for j in range(n_seq):
+        kv_at = pl.ds(pl.multiple_of(seq_to[j] * size, size), size)
+        kv_part[j] = jnp.dot(xs_scr[...], wkv_buf[:, kv_at], preferred_element_type=f32)
     kv_copies = []
     for j in range(n_seq - 1):
         copy = to("seq", seq_to[j], kv_part.at[j], kv_buf.at[slots[j]], kv_send.at[j], kv_recv.at[slots[j]])
@@ -296,6 +295,17 @@
     stats = soften(kv_head, stats)
     if kv > 1:
         accumulate(kv_head)
+    new_part = kv_part[n_seq - 1]
+    for copy in kv_copies:
+        copy.wait_recv()
+    for j in range(n_seq - 1):
+        new_part = new_part + kv_buf[j]
+    nk_buf[seq] = (new_part * inverse_rms).astype(bf16)
+    nk_copies = []
+    for j in range(n_seq - 1):
+        copy = to("seq", seq_to[j], nk_buf.at[seq], nk_buf.at[seq], nk_send.at[j], nk_recv.at[slots[j]])
+        copy.start()
+        nk_copies.append(copy)
     others = [lax.rem(kv_head + t, kv) for t in range(1, kv)]
     for k in others:
         for t in range(sources):
@@ -308,17 +318,6 @@
         copy = to("seq", seq_to[j], st_buf.at[n_seq - 1], st_buf.at[slots[j]], st_send.at[j], st_recv.at[slots[j]])
         copy.start()
         st_copies.append(copy)
-    new_part = kv_part[n_seq - 1]
-    for copy in kv_copies:
-        copy.wait_recv()
-    for j in range(n_seq - 1):
-        new_part = new_part + kv_buf[j]
-    nk_buf[seq] = (new_part * inverse_rms).astype(bf16)
-    nk_copies = []
-    for j in range(n_seq - 1):
-        copy = to("seq", seq_to[j], nk_buf.at[seq], nk_buf.at[seq], nk_send.at[j], nk_recv.at[slots[j]])
-        copy.start()
-        nk_copies.append(copy)
     for k in others if kv > 1 else [kv_head]:
         accumulate(k)
 

time: 44.9 us -> 44.6 us (level)
  no operation moved by 1% of the time
where the time goes in v5:
time: 44.6 us; the launch traced here: 44.3 us
  Pallas kernels  42.9 us (96%)
  local copies, waits for them, and re-layouts  1.42 us (3%)
    pallas_call x1, Pallas kernels, fused(): pl.pallas_call(functools.partial(layer_kernel, n_seq, n_head), out_shape=...  42.9 us
    unnamed x1, local copies, waits for them, and re-layouts  1.42 us

profile of v5, /device:TPU:0, one launch (start us, length us, event | category | flops | bytes accessed | tf_op | source)
XLA Modules:
  0.0 44.3 jit_solution(17737550247398738955)
XLA Ops:
  0.0 42.9 %shard_map.91 = bf16[6,3072]{1,0:T(8,128)(2,1)} custom-call(bf16[6,3072]{1,0:T(8,128)(2,1)} %hid.1, f32[1,3072]{1,0:T(1,128)} %bitcast.1, s32[24]{0:T(128)} %lens.1, bf16[3072,3072]{1,0:T(8,128)(2,1)} %wq.1, bf16[3072,256]{1,0:T(8,128)(2,1)} %wk.1, bf16[3072,256]{1,0:T(8,128)(2,1)} %wv.1, bf16[3072,3072]{1,0:T(8,128)(2,1)} %wo.1, ...), custom_call_target="tpu_custom_call" | custom-call | tf_op jit(solution)/shard_map/pallas_call | solution.py:458
  42.9 1.4 %copy.11 = bf16[6,3072]{1,0:T(8,128)(2,1)} copy(bf16[6,3072]{1,0:T(8,128)(2,1)} %shard_map.91) | data formatting | bytes 73728
